TPU v7x, 32 devices: a whole 2x2x4 slice. The times are simulated.
32 devices in a mesh: dp: 4 (over z), ctx: 4 (over x, core), uly: 2 (over y).
Axes of the slice: x: 2, y: 2, z: 4, core: 2. Of those that a mesh axis runs over, the one named last changes fastest.
Arguments:
- queries: bfloat16 [4096, 4096], P(('dp', 'ctx', 'uly')), parts along dimension 0, may hold values from -130 to 130
- keys: bfloat16 [4096, 1024], P(('dp', 'ctx', 'uly')), parts along dimension 0, may hold values from -6.5 to 6.5
- values: bfloat16 [4096, 1024], P(('dp', 'ctx', 'uly')), parts along dimension 0, may hold values from -6 to 6
- d_out: bfloat16 [4096, 4096], P(('dp', 'ctx', 'uly')), parts along dimension 0, may hold values from -96 to 96
- rand_blocks: int32 [32, 3], P('dp'), parts along dimension 0, may hold values from 0 to 7, as said below
Outputs:
- d_queries: bfloat16 [4096, 4096], P(('dp', 'ctx', 'uly')), parts along dimension 0
- d_keys: bfloat16 [4096, 1024], P(('dp', 'ctx', 'uly')), parts along dimension 0
- d_values: bfloat16 [4096, 1024], P(('dp', 'ctx', 'uly')), parts along dimension 0
There are 4 independent parts, one for each index of `dp`. A program takes and returns all parts, laid end to end along the dimension named above; each array names one. Nothing has to cross between parts.
Inputs may be any that keep to these rules, and one draw needn't show every extreme that they name: `rand_blocks`: for every group of 2 consecutive query blocks, the entries of its lists (window, random) that name blocks of one other group of 2 number at most 2, and at most 4 when the 2 global blocks are counted once each; both bounds are reached in every draw.
All inputs are finite; a program needn't handle non-finite values.
Results may differ from a plain program's by a relative error of at most 0.005.
Values may be sent and summed in bfloat16 or wider, within the bound.
No kernel may reach another device: no remote copies, remote signals or barrier semaphores. Data moves between devices by JAX's collectives and lax.ppermute only.
A program may use at most 128 MiB of HBM per device.

v0:
```python
from functools import partial
import jax
import jax.numpy as jnp
from jax import lax
from jax.sharding import PartitionSpec as P

HEAD_DIM = 128
BLOCK = 128
WINDOW = 3
GLOBALS = 2
RANDOMS = 3
ENTRIES = 8
GROUP = 4


def listed_blocks(rand_blocks):
    total = rand_blocks.shape[0]
    block_ids = jnp.arange(total, dtype=jnp.int32)
    window_part = (
        block_ids[:, None] + jnp.arange(WINDOW, dtype=jnp.int32)[None, :] - WINDOW // 2
    ) % total
    global_part = jnp.broadcast_to(jnp.arange(GLOBALS, dtype=jnp.int32)[None, :], (total, GLOBALS))
    return jnp.concatenate([window_part, global_part, rand_blocks], axis=1)


def block_backward(sources, softmax_scale, inputs):
    query_blk, dout_blk, source_rows = inputs
    picked = jnp.take(sources, source_rows, axis=0)
    kv_width = picked.shape[-1] // 2
    kv_count = kv_width // HEAD_DIM
    key_sel = picked[..., :kv_width].reshape(ENTRIES, BLOCK, kv_count, HEAD_DIM)
    value_sel = picked[..., kv_width:].reshape(ENTRIES, BLOCK, kv_count, HEAD_DIM)
    query_four = query_blk.reshape(BLOCK, kv_count, GROUP, HEAD_DIM)
    dout_four = dout_blk.reshape(BLOCK, kv_count, GROUP, HEAD_DIM)
    scores = jnp.einsum("tkgd,eskd->kgtes", query_four, key_sel, preferred_element_type=jnp.float32)
    scores = scores.reshape(kv_count, GROUP, BLOCK, ENTRIES * BLOCK) * softmax_scale
    row_max = jnp.max(scores, axis=-1, keepdims=True)
    exp_scores = jnp.exp(scores - row_max)
    prob_rows = exp_scores / jnp.sum(exp_scores, axis=-1, keepdims=True)
    grad_probs = jnp.einsum(
        "tkgd,eskd->kgtes", dout_four, value_sel, preferred_element_type=jnp.float32
    )
    grad_probs = grad_probs.reshape(kv_count, GROUP, BLOCK, ENTRIES * BLOCK)
    row_delta = jnp.sum(prob_rows * grad_probs, axis=-1, keepdims=True)
    grad_scores = (
        (prob_rows * (grad_probs - row_delta))
        .astype(jnp.bfloat16)
        .reshape(kv_count, GROUP, BLOCK, ENTRIES, BLOCK)
    )
    probs_low = prob_rows.astype(jnp.bfloat16).reshape(kv_count, GROUP, BLOCK, ENTRIES, BLOCK)
    grad_values = jnp.einsum(
        "kgtes,tkgd->eskd", probs_low, dout_four, preferred_element_type=jnp.float32
    )
    grad_keys = (
        jnp.einsum("kgtes,tkgd->eskd", grad_scores, query_four, preferred_element_type=jnp.float32)
        * softmax_scale
    )
    grad_query = (
        jnp.einsum("kgtes,eskd->tkgd", grad_scores, key_sel, preferred_element_type=jnp.float32)
        * softmax_scale
    )
    partials = jnp.concatenate(
        [
            grad_keys.reshape(ENTRIES, BLOCK, kv_width),
            grad_values.reshape(ENTRIES, BLOCK, kv_width),
        ],
        axis=-1,
    )
    return (partials, grad_query.reshape(BLOCK, kv_count * GROUP * HEAD_DIM))


def per_device(queries, keys, values, d_out, rand_blocks):
    softmax_scale = HEAD_DIM ** (-0.5)
    groups = lax.axis_size("ctx")
    my_group = lax.axis_index("ctx")
    queries_here, dout_here, keys_here, values_here = (
        lax.all_to_all(queries, "uly", split_axis=1, concat_axis=0, tiled=True),
        lax.all_to_all(d_out, "uly", split_axis=1, concat_axis=0, tiled=True),
        lax.all_to_all(keys, "uly", split_axis=1, concat_axis=0, tiled=True),
        lax.all_to_all(values, "uly", split_axis=1, concat_axis=0, tiled=True),
    )
    tokens_here = keys_here.shape[0]
    per_group = tokens_here // BLOCK
    kv_width = keys_here.shape[1]
    local_blocks = jnp.concatenate([keys_here, values_here], axis=1).reshape(
        per_group, BLOCK, 2 * kv_width
    )
    listed = listed_blocks(rand_blocks)
    owners = listed // per_group
    offsets = listed % per_group
    requester = (jnp.arange(listed.shape[0], dtype=jnp.int32) // per_group)[:, None]
    entry_ids = jnp.arange(ENTRIES, dtype=jnp.int32)
    is_global = (entry_ids >= WINDOW) & (entry_ids < WINDOW + GLOBALS)
    entry_global = jnp.tile(is_global, per_group)
    global_slot = jnp.tile(entry_ids - WINDOW, per_group)
    rand_capacity = per_group * RANDOMS // groups + 1
    remote = owners != requester
    capacity = rand_capacity + GLOBALS
    lead_slots = GLOBALS
    owners = owners.reshape(groups, per_group * ENTRIES)
    offsets = offsets.reshape(groups, per_group * ENTRIES)
    remote = remote.reshape(groups, per_group * ENTRIES)
    counted = remote & jnp.logical_not(entry_global)[None, :]
    owner_hot = (
        (owners[:, :, None] == jnp.arange(groups, dtype=jnp.int32)[None, None, :])
        & counted[:, :, None]
    ).astype(jnp.int32)
    rand_slot = jnp.sum((jnp.cumsum(owner_hot, axis=1) - 1) * owner_hot, axis=2) + lead_slots
    slot_index = jnp.where(entry_global[None, :], global_slot[None, :], rand_slot)
    for_me = remote & (owners == my_group)
    slot_match = (
        slot_index[:, :, None, None] == jnp.arange(capacity, dtype=jnp.int32)[None, None, :, None]
    )
    block_match = (
        offsets[:, :, None, None] == jnp.arange(per_group, dtype=jnp.int32)[None, None, None, :]
    )
    slot_picker = jnp.minimum(
        jnp.sum((for_me[:, :, None, None] & slot_match & block_match).astype(jnp.int32), axis=1), 1
    )
    outgoing = jnp.einsum(
        "csb,bxd->csxd",
        slot_picker.astype(jnp.bfloat16),
        local_blocks,
        preferred_element_type=jnp.float32,
    ).astype(jnp.bfloat16)
    incoming = lax.all_to_all(outgoing, "ctx", split_axis=0, concat_axis=0, tiled=True)
    my_owner = lax.dynamic_index_in_dim(owners, my_group, 0, keepdims=False)
    my_slot = lax.dynamic_index_in_dim(slot_index, my_group, 0, keepdims=False)
    my_offset = lax.dynamic_index_in_dim(offsets, my_group, 0, keepdims=False)
    my_remote = lax.dynamic_index_in_dim(remote, my_group, 0, keepdims=False)
    source_rows = jnp.where(my_remote, per_group + my_owner * capacity + my_slot, my_offset)
    pieces = [local_blocks, incoming.reshape(groups * capacity, BLOCK, 2 * kv_width)]
    sources = jnp.concatenate(pieces, axis=0)
    source_count = sources.shape[0]
    query_blocks = queries_here.reshape(per_group, BLOCK, queries_here.shape[1])
    dout_blocks = dout_here.reshape(per_group, BLOCK, dout_here.shape[1])
    partials, grad_query = lax.map(
        partial(block_backward, sources, softmax_scale),
        (query_blocks, dout_blocks, source_rows.reshape(per_group, ENTRIES)),
    )
    source_hot = (
        source_rows[:, None] == jnp.arange(source_count, dtype=jnp.int32)[None, :]
    ).astype(jnp.float32)
    source_grads = jnp.einsum(
        "ms,mxd->sxd",
        source_hot,
        partials.reshape(per_group * ENTRIES, BLOCK, 2 * kv_width),
        precision=lax.Precision.HIGHEST,
    )
    own_grads = source_grads[:per_group]
    sent_grads = source_grads[per_group : per_group + groups * capacity].reshape(
        groups, capacity, BLOCK, 2 * kv_width
    )
    returned = lax.all_to_all(sent_grads, "ctx", split_axis=0, concat_axis=0, tiled=True)
    own_grads = own_grads + jnp.einsum(
        "csb,csxd->bxd", slot_picker.astype(jnp.float32), returned, precision=lax.Precision.HIGHEST
    )
    query_grads = grad_query.reshape(tokens_here, queries_here.shape[1]).astype(jnp.bfloat16)
    key_grads = own_grads[..., :kv_width].reshape(tokens_here, kv_width).astype(jnp.bfloat16)
    value_grads = own_grads[..., kv_width:].reshape(tokens_here, kv_width).astype(jnp.bfloat16)
    d_queries, d_keys, d_values = (
        lax.all_to_all(query_grads, "uly", split_axis=0, concat_axis=1, tiled=True),
        lax.all_to_all(key_grads, "uly", split_axis=0, concat_axis=1, tiled=True),
        lax.all_to_all(value_grads, "uly", split_axis=0, concat_axis=1, tiled=True),
    )
    return (d_queries, d_keys, d_values)


def solution(mesh):
    in_specs = (
        P(("dp", "ctx", "uly"), None),
        P(("dp", "ctx", "uly"), None),
        P(("dp", "ctx", "uly"), None),
        P(("dp", "ctx", "uly"), None),
        P("dp", None),
    )
    out_specs = (
        P(("dp", "ctx", "uly"), None),
        P(("dp", "ctx", "uly"), None),
        P(("dp", "ctx", "uly"), None),
    )
    return jax.shard_map(
        per_device, mesh=mesh, in_specs=in_specs, out_specs=out_specs, check_vma=False
    )
```

profile of v0, /device:TPU:0, one launch (start us, length us, event | category | flops | bytes accessed | tf_op | source)
XLA Modules:
  0.0 362.4 jit_solution(10996990037546857192)
XLA Ops:
  2.6 4.2 %all-to-all-start.2 = ((bf16[128,2,512]{2,0,1:T(8,128)(2,1)}), bf16[128,2,512]{2,0,1:T(8,128)(2,1)S(1)}, u32[]{:S(2)}, u32[]{:S(2)}) async-start(bf16[128,2,512]{2,0,1:T(8,128)(2,1)} %copy.130), calls=%async_computation.2 | async-start | bytes 524288 | tf_op jit(solution)/shard_map/all_to_all | solution.py:80
  12.7 3.5 all-to-all-start.1
  16.2 5.8 %all-to-all-done.1 = bf16[128,2,512]{2,0,1:T(8,128)(2,1)S(1)} async-done(((bf16[128,2,512]{2,0,1:T(8,128)(2,1)}), bf16[128,2,512]{2,0,1:T(8,128)(2,1)S(1)}, u32[]{:S(2)}, u32[]{:S(2)}) %all-to-all-start.1) | async-done | bytes 262176 | tf_op jit(solution)/shard_map/all_to_all | solution.py:79
  22.1 4.4 %all-to-all-start = ((bf16[128,2,2048]{0,2,1:T(8,128)(2,1)}), bf16[128,2,2048]{0,2,1:T(8,128)(2,1)}, u32[]{:S(2)}, u32[]{:S(2)}) async-start(bf16[128,2,2048]{0,2,1:T(8,128)(2,1)} %bitcast.31), calls=%async_computation | async-start | bytes 2097152 | tf_op jit(solution)/shard_map/all_to_all | solution.py:77
  27.4 4.4 %convolution_convert_fusion = bf16[4,4,128,1024]{3,1,2,0:T(4,128)(2,1)} fusion(s32[4,4,2]{1,2,0:T(2,128)S(1)} %convert_reduce_fusion, bf16[2,128,512]{2,0,1:T(2,128)(2,1)S(1)} %bitcast.211, bf16[2,128,512]{2,0,1:T(2,128)(2,1)S(1)} %bitcast.213), kind=kOutput, calls=%fused_computation.38 | convolution fusion | flops 11534400 | bytes 4718720 | tf_op jit(solution)/shard_map/csb,bxd->csxd/dot_general | solution.py:120
  31.8 8.1 %all-to-all-done = bf16[128,2,2048]{0,2,1:T(8,128)(2,1)} async-done(((bf16[128,2,2048]{0,2,1:T(8,128)(2,1)}), bf16[128,2,2048]{0,2,1:T(8,128)(2,1)}, u32[]{:S(2)}, u32[]{:S(2)}) %all-to-all-start) | async-done | bytes 1048608 | tf_op jit(solution)/shard_map/all_to_all | solution.py:77
  39.9 4.9 %all-to-all-start.3 = ((bf16[4,4,128,1024]{3,1,2,0:T(4,128)(2,1)}), bf16[4,4,128,1024]{3,1,2,0:T(4,128)(2,1)}, u32[]{:S(2)}, u32[]{:S(2)}) async-start(bf16[4,4,128,1024]{3,1,2,0:T(4,128)(2,1)} %convolution_convert_fusion), calls=%async_computation.3 | async-start | bytes 8388608 | tf_op jit(solution)/shard_map/all_to_all | solution.py:126
  46.2 46.9 %all-to-all-done.3 = bf16[4,4,128,1024]{3,1,2,0:T(4,128)(2,1)} async-done(((bf16[4,4,128,1024]{3,1,2,0:T(4,128)(2,1)}), bf16[4,4,128,1024]{3,1,2,0:T(4,128)(2,1)}, u32[]{:S(2)}, u32[]{:S(2)}) %all-to-all-start.3) | async-done | bytes 4194336 | tf_op jit(solution)/shard_map/all_to_all | solution.py:126
  93.1 4.4 %all-to-all-start.4 = ((bf16[128,2,2048]{0,2,1:T(8,128)(2,1)}), bf16[128,2,2048]{0,2,1:T(8,128)(2,1)}, u32[]{:S(2)}, u32[]{:S(2)}) async-start(bf16[128,2,2048]{0,2,1:T(8,128)(2,1)} %bitcast.41), calls=%async_computation.4 | async-start | bytes 2097152 | tf_op jit(solution)/shard_map/all_to_all | solution.py:78
  99.9 3.6 %copy.132 = bf16[4,4,128,1024]{3,2,1,0:T(8,128)(2,1)S(1)} copy(bf16[4,4,128,1024]{3,1,2,0:T(4,128)(2,1)} %all-to-all-done.3) | data formatting | bytes 8388608 | tf_op jit(solution)/shard_map/all_to_all | solution.py:126
  106.1 5.2 %all-to-all-done.4 = bf16[128,2,2048]{0,2,1:T(8,128)(2,1)} async-done(((bf16[128,2,2048]{0,2,1:T(8,128)(2,1)}), bf16[128,2,2048]{0,2,1:T(8,128)(2,1)}, u32[]{:S(2)}, u32[]{:S(2)}) %all-to-all-start.4) | async-done | bytes 1048608 | tf_op jit(solution)/shard_map/all_to_all | solution.py:78
  111.3 65.8 %while.12 = (s32[]{:T(128)}, f32[2,8,128,1024]{2,3,1,0:T(8,128)}, bf16[2,128,2048]{1,2,0:T(8,128)(2,1)}, bf16[2,128,2048]{1,2,0:T(8,128)(2,1)}, s32[2,8]{1,0:T(2...) while((s32[]{:T(128)}, f32[2,8,128,1024]{2,3,1,0:T(8,128)}, ...), condition=%wide.region_7.8_spmd, body=%wide.region_3.7_spmd.sunk | while | flops 2729438208 | bytes 243889072 | solution.py:137
  126.1 5.3 %fusion.92 = (f32[4,4,128]{2,1,0:T(4,128)S(1)}, f32[4,8,128,128,4]{3,2,4,1,0:T(8,128)S(1)}) fusion(f32[4,4,128]{2,1,0:T(4,128)S(1)} %fusion.90, f32[4,4,128]{2,1,0:T(4,128)S(1)} %get-tuple-element.135, f32[4,8,128,128,4]{3,2,4,1,0:T(8,128)} %copy-done, bf16[128,4,4,128,1]{0,3,2,4,1:T(8,128)(2,1)S(1)} %bitcast.200, ...), kind=kOutput, calls=%fused_computation.3.clone.1 | convolution fusion | flops 547354624 | bytes 18374656 | tf_op jit(solution)/shard_map/while/body/eval_jaxpr/tkgd,eskd->kgtes/dot_general | solution.py:40
  159.0 5.3 %fusion.92 = (f32[4,4,128]{2,1,0:T(4,128)S(1)}, f32[4,8,128,128,4]{3,2,4,1,0:T(8,128)S(1)}) fusion(f32[4,4,128]{2,1,0:T(4,128)S(1)} %fusion.90, f32[4,4,128]{2,1,0:T(4,128)S(1)} %get-tuple-element.135, f32[4,8,128,128,4]{3,2,4,1,0:T(8,128)} %copy-done, bf16[128,4,4,128,1]{0,3,2,4,1:T(8,128)(2,1)S(1)} %bitcast.200, ...), kind=kOutput, calls=%fused_computation.3.clone.1 | convolution fusion | flops 547354624 | bytes 18374656 | tf_op jit(solution)/shard_map/while/body/eval_jaxpr/tkgd,eskd->kgtes/dot_general | solution.py:40
  177.1 8.9 %copy.136 = f32[16,128,1024]{2,0,1:T(8,128)} copy(f32[16,128,1024]{1,2,0:T(8,128)} %bitcast.205) | data formatting | bytes 16777216 | tf_op jit(solution)/shard_map/reshape | solution.py:147
  186.0 9.6 %fusion.35 = f32[18,128,1024]{2,0,1:T(8,128)S(1)} fusion(f32[16,128,1024]{2,0,1:T(8,128)} %copy.136, s32[16]{0:T(128)S(1)} %bitcast.215), kind=kOutput, calls=%fused_computation.55 | convolution fusion | flops 452985120 | bytes 17825856 | tf_op jit(solution)/shard_map/ms,mxd->sxd/dot_general | solution.py:144
  195.6 4.5 %copy-done.2 = f32[18,128,1024]{2,0,1:T(8,128)} copy-done((f32[18,128,1024]{2,0,1:T(8,128)}, f32[18,128,1024]{2,0,1:T(8,128)S(1)}, u32[]{:S(2)}) %copy-start.2) | copy-done | bytes 9437208
  200.1 5.3 %slice.29 = f32[16,128,1024]{2,0,1:T(8,128)} slice(f32[18,128,1024]{2,0,1:T(8,128)S(1)} %fusion.35), slice={[2:18], [0:128], [0:1024]} | slice | bytes 16777216 | tf_op jit(solution)/shard_map/slice | solution.py:151
  205.4 9.8 %reshape.355 = f32[4,4,128,1024]{3,1,0,2:T(4,128)} reshape(f32[16,128,1024]{2,0,1:T(8,128)} %slice.29) | data formatting | bytes 16777216 | tf_op jit(solution)/shard_map/reshape | solution.py:151
  215.2 9.4 %copy.137 = f32[4,4,128,1024]{3,1,2,0:T(4,128)} copy(f32[4,4,128,1024]{3,1,0,2:T(4,128)} %reshape.355) | data formatting | bytes 16777216 | tf_op jit(solution)/shard_map/reshape | solution.py:151
  224.7 100.7 %all_to_all.122 = f32[4,4,128,1024]{3,1,2,0:T(4,128)} all-to-all(f32[4,4,128,1024]{3,1,2,0:T(4,128)} %copy.137), channel_id=1, replica_groups=mesh['dp'=4,'ctx'=4,'uly'=2] {'ctx'}, dimensions={0} | all-to-all | bytes 16777216 | tf_op jit(solution)/shard_map/all_to_all | solution.py:154
  325.3 3.6 all-to-all-start.5
  328.9 14.1 %fusion.29 = bf16[2,128,1024]{2,0,1:T(2,128)(2,1)S(1)} fusion(f32[4,4,128,1024]{3,1,2,0:T(4,128)} %all_to_all.122, f32[18,128,1024]{2,0,1:T(8,128)} %copy-done.2, s32[4,4,2]{1,2,0:T(2,128)S(1)} %copy-done.6), kind=kOutput, calls=%fused_computation.41 | convolution fusion | flops 50856000 | bytes 9961600 | tf_op jit(solution)/shard_map/csb,csxd->bxd/dot_general | solution.py:155
  348.3 4.4 %all-to-all-done.7 = bf16[2,128,512]{2,1,0:T(8,128)(2,1)S(1)} async-done(((bf16[2,128,512]{2,1,0:T(8,128)(2,1)}), bf16[2,128,512]{2,1,0:T(8,128)(2,1)S(1)}, u32[]{:S(2)}, u32[]{:S(2)}) %all-to-all-start.7) | async-done | bytes 262176 | tf_op jit(solution)/shard_map/all_to_all | solution.py:163
  (122 shorter events, 84.6 us)
Async XLA Ops:
  2.6 10.1 %all-to-all-start.2 = ((bf16[128,2,512]{2,0,1:T(8,128)(2,1)}), bf16[128,2,512]{2,0,1:T(8,128)(2,1)S(1)}, u32[]{:S(2)}, u32[]{:S(2)}) async-start(bf16[128,2,512]{2,0,1:T(8,128)(2,1)} %copy.130), calls=%async_computation.2 | async-start | bytes 524288 | tf_op jit(solution)/shard_map/all_to_all | solution.py:80
  12.7 9.3 %all-to-all-start.1 = ((bf16[128,2,512]{2,0,1:T(8,128)(2,1)}), bf16[128,2,512]{2,0,1:T(8,128)(2,1)S(1)}, u32[]{:S(2)}, u32[]{:S(2)}) async-start(bf16[128,2,512]{2,0,1:T(8,128)(2,1)} %copy.127), calls=%async_computation.1 | async-start | bytes 524288 | tf_op jit(solution)/shard_map/all_to_all | solution.py:79
  16.2 28.6 %copy-start.4 = (bf16[128,4096]{1,0:T(8,128)(2,1)S(1)}, bf16[128,4096]{1,0:T(8,128)(2,1)}, u32[]{:S(2)}) copy-start(bf16[128,4096]{1,0:T(8,128)(2,1)} %param.10) | copy-start | bytes 3145732
  22.1 17.8 %all-to-all-start = ((bf16[128,2,2048]{0,2,1:T(8,128)(2,1)}), bf16[128,2,2048]{0,2,1:T(8,128)(2,1)}, u32[]{:S(2)}, u32[]{:S(2)}) async-start(bf16[128,2,2048]{0,2,1:T(8,128)(2,1)} %bitcast.31), calls=%async_computation | async-start | bytes 2097152 | tf_op jit(solution)/shard_map/all_to_all | solution.py:77
  26.7 0.6 copy-start.5
  39.9 53.2 %all-to-all-start.3 = ((bf16[4,4,128,1024]{3,1,2,0:T(4,128)(2,1)}), bf16[4,4,128,1024]{3,1,2,0:T(4,128)(2,1)}, u32[]{:S(2)}, u32[]{:S(2)}) async-start(bf16[4,4,128,1024]{3,1,2,0:T(4,128)(2,1)} %convolution_convert_fusion), calls=%async_computation.3 | async-start | bytes 8388608 | tf_op jit(solution)/shard_map/all_to_all | solution.py:126
  93.1 18.2 %all-to-all-start.4 = ((bf16[128,2,2048]{0,2,1:T(8,128)(2,1)}), bf16[128,2,2048]{0,2,1:T(8,128)(2,1)}, u32[]{:S(2)}, u32[]{:S(2)}) async-start(bf16[128,2,2048]{0,2,1:T(8,128)(2,1)} %bitcast.41), calls=%async_computation.4 | async-start | bytes 2097152 | tf_op jit(solution)/shard_map/all_to_all | solution.py:78
  120.1 3.2 copy-start
  126.1 6.1 %copy-start.1 = (f32[4,8,128,128,4]{3,2,4,1,0:T(8,128)S(1)}, f32[4,8,128,128,4]{3,2,4,1,0:T(8,128)}, u32[]{:S(2)}) copy-start(f32[4,8,128,128,4]{3,2,4,1,0:T(8,128)} %copy-done) | copy-start | bytes 25165828 | tf_op jit(solution)/shard_map/while
  136.1 2.6 slice-start
  136.3 3.4 slice-start.1
  140.1 3.2 copy-start.3
  153.0 3.2 copy-start
  159.0 6.1 %copy-start.1 = (f32[4,8,128,128,4]{3,2,4,1,0:T(8,128)S(1)}, f32[4,8,128,128,4]{3,2,4,1,0:T(8,128)}, u32[]{:S(2)}) copy-start(f32[4,8,128,128,4]{3,2,4,1,0:T(8,128)} %copy-done) | copy-start | bytes 25165828 | tf_op jit(solution)/shard_map/while
  169.0 2.6 slice-start
  169.2 3.4 slice-start.1
  173.0 3.2 copy-start.3
  177.1 8.9 %copy-start.7 = (s32[1,16]{1,0:T(1,128)S(1)}, s32[1,16]{1,0:T(1,128)}, u32[]{:S(2)}) copy-start(s32[1,16]{1,0:T(1,128)} %get-tuple-element.67) | copy-start | bytes 196
  195.6 4.5 %copy-start.2 = (f32[18,128,1024]{2,0,1:T(8,128)}, f32[18,128,1024]{2,0,1:T(8,128)S(1)}, u32[]{:S(2)}) copy-start(f32[18,128,1024]{2,0,1:T(8,128)S(1)} %fusion.35) | copy-start | bytes 28311556
  224.7 104.3 %copy-start.6 = (s32[4,4,2]{1,2,0:T(2,128)S(1)}, s32[4,4,2]{1,2,0:T(2,128)}, u32[]{:S(2)}) copy-start(s32[4,4,2]{1,2,0:T(2,128)} %copy-done.5) | copy-start | bytes 388
  325.3 18.8 %all-to-all-start.5 = ((bf16[2,128,2048]{1,2,0:T(8,128)(2,1)}), bf16[2,128,2048]{1,2,0:T(8,128)(2,1)S(1)}, u32[]{:S(2)}, u32[]{:S(2)}) async-start(bf16[2,128,2048]{1,2,0:T(8,128)(2,1)} %get-tuple-element.41), calls=%async_computation.5 | async-start | bytes 2097152 | tf_op jit(solution)/shard_map/all_to_all | solution.py:162
  344.1 8.6 %all-to-all-start.7 = ((bf16[2,128,512]{2,1,0:T(8,128)(2,1)}), bf16[2,128,512]{2,1,0:T(8,128)(2,1)S(1)}, u32[]{:S(2)}, u32[]{:S(2)}) async-start(bf16[2,128,512]{2,1,0:T(8,128)(2,1)} %copy.139), calls=%async_computation.7 | async-start | bytes 524288 | tf_op jit(solution)/shard_map/all_to_all | solution.py:163
  352.7 8.6 %all-to-all-start.8 = ((bf16[2,128,512]{2,1,0:T(8,128)(2,1)}), bf16[2,128,512]{2,1,0:T(8,128)(2,1)S(1)}, u32[]{:S(2)}, u32[]{:S(2)}) async-start(bf16[2,128,512]{2,1,0:T(8,128)(2,1)} %copy.141), calls=%async_computation.8 | async-start | bytes 524288 | tf_op jit(solution)/shard_map/all_to_all | solution.py:164
where the time goes:
time: 364 us; the launch traced here: 362 us
  blocking collectives  101 us (28%)
  local copies, waits for them, and re-layouts  90.3 us (25%)
  waiting for transfers between devices  73.3 us (20%)
  matrix products  50.2 us (14%)
  starting transfers between devices  31.9 us (9%)
  other arithmetic  14.7 us (4%)
    all_to_all x1, blocking collectives, per_device(): lax.all_to_all(sent_grads, 'ctx', split_axis=0, concat_axis=0, tiled=True)  101 us
    all_to_all x1, waiting for transfers between devices, per_device(): lax.all_to_all(outgoing, 'ctx', split_axis=0, concat_axis=0, tiled=True)  46.9 us
    reshape x2, local copies, waits for them, and re-layouts, per_device(): source_grads[per_group:per_group + groups * capacity]  19.2 us
    while x20, local copies, waits for them, and re-layouts  14.9 us
    dot_general x1, matrix products, per_device(): jnp.einsum('csb,csxd->bxd', slot_picker.astype(jnp.float32), returned, pr...  14.1 us
    unnamed x16, local copies, waits for them, and re-layouts  12.1 us
    dot_general x2, matrix products, block_backward(): jnp.einsum('tkgd,eskd->kgtes', dout_four, value_sel, preferred_element_ty...  10.7 us
    dot_general x1, matrix products, per_device(): jnp.einsum('ms,mxd->sxd', source_hot, partials.reshape(per_group * ENTRIE...  9.64 us
  transfers between devices with their start and end apart: 8, of which 6 were waited for; matrix products, arithmetic and copies ran while one was open for 11% of the time, Pallas kernels for 0%

commit v1 on v0

--- a/solution.py
+++ b/solution.py
@@ -123,7 +123,19 @@
         local_blocks,
         preferred_element_type=jnp.float32,
     ).astype(jnp.bfloat16)
-    incoming = lax.all_to_all(outgoing, "ctx", split_axis=0, concat_axis=0, tiled=True)
+    ways, here = (lax.axis_size("ctx"), lax.axis_index("ctx"))
+    width = outgoing.shape[0] // ways
+    dims = list(outgoing.shape)
+    dims[0] = width
+    height = dims[0]
+    dims[0] = height * ways
+    full = jnp.zeros(dims, outgoing.dtype)
+    for mask in range(ways):
+        part = lax.dynamic_slice_in_dim(outgoing, (here ^ mask) * width, width, axis=0)
+        if mask:
+            part = lax.ppermute(part, "ctx", [(d, d ^ mask) for d in range(ways)])
+        full = lax.dynamic_update_slice_in_dim(full, part, (here ^ mask) * height, axis=0)
+    incoming = full
     my_owner = lax.dynamic_index_in_dim(owners, my_group, 0, keepdims=False)
     my_slot = lax.dynamic_index_in_dim(slot_index, my_group, 0, keepdims=False)
     my_offset = lax.dynamic_index_in_dim(offsets, my_group, 0, keepdims=False)

time: 364 us -> 335 us (0.920)
  waiting for transfers between devices: 73.3 us -> 35.4 us
  local copies, waits for them, and re-layouts: 90.3 us -> 104 us
    all_to_all x1 -> x0, waiting for transfers between devices: 46.9 us -> none  [per_device(): lax.all_to_all(outgoing, 'ctx', split_axis=0, concat_axis=0, tiled=True)]
    ppermute x0 -> x3, waiting for transfers between devices: none -> 14.1 us  [per_device(): part = lax.ppermute(part, 'ctx', [(d, d ^ mask) for d in range(ways)])]
    dynamic_update_slice x0 -> x4, local copies, waits for them, and re-layouts: none -> 10.4 us  [per_device(): lax.dynamic_update_slice_in_dim(full, part, (here ^ mask) * height, axis=0)]
    all_to_all x1, waiting for transfers between devices: 5.16 us -> 0.01 us  [per_device(): lax.all_to_all(d_out, 'uly', split_axis=1, concat_axis=0, tiled=True)]
    all_to_all x1 -> x0, starting transfers between devices: 4.93 us -> none  [per_device(): lax.all_to_all(outgoing, 'ctx', split_axis=0, concat_axis=0, tiled=True)]
    unnamed x16 -> x14, local copies, waits for them, and re-layouts: 12.1 us -> 13 us
  transfers between devices with their start and end apart: 8 -> 10, of which waited for: 6 -> 6; matrix products, arithmetic and copies ran while one was open for 11% -> 13% of each run, Pallas kernels for 0% -> 0%
where the time goes in v1:
time: 335 us; the launch traced here: 334 us
  local copies, waits for them, and re-layouts  104 us (31%)
  blocking collectives  101 us (30%)
  matrix products  48.7 us (15%)
  waiting for transfers between devices  35.4 us (11%)
  starting transfers between devices  28.9 us (9%)
  other arithmetic  14.6 us (4%)
    all_to_all x1, blocking collectives, per_device(): lax.all_to_all(sent_grads, 'ctx', split_axis=0, concat_axis=0, tiled=True)  101 us
    reshape x2, local copies, waits for them, and re-layouts, per_device(): source_grads[per_group:per_group + groups * capacity]  19.2 us
    while x20, local copies, waits for them, and re-layouts  14.9 us
    ppermute x3, waiting for transfers between devices, per_device(): part = lax.ppermute(part, 'ctx', [(d, d ^ mask) for d in range(ways)])  14.1 us
    dot_general x1, matrix products, per_device(): jnp.einsum('csb,csxd->bxd', slot_picker.astype(jnp.float32), returned, pr...  14.1 us
    unnamed x14, local copies, waits for them, and re-layouts  13 us
    dot_general x2, matrix products, block_backward(): jnp.einsum('tkgd,eskd->kgtes', dout_four, value_sel, preferred_element_ty...  10.7 us
    dynamic_update_slice x4, local copies, waits for them, and re-layouts, per_device(): lax.dynamic_update_slice_in_dim(full, part, (here ^ mask) * height, axis=0)  10.4 us
  transfers between devices with their start and end apart: 10, of which 6 were waited for; matrix products, arithmetic and copies ran while one was open for 13% of the time, Pallas kernels for 0%

profile of v1, /device:TPU:0, one launch (start us, length us, event | category | flops | bytes accessed | tf_op | source)
XLA Modules:
  0.0 333.7 jit_solution(9683864671505907872)
XLA Ops:
  2.6 4.2 %all-to-all-start.2 = ((bf16[128,2,512]{2,0,1:T(8,128)(2,1)}), bf16[128,2,512]{2,0,1:T(8,128)(2,1)S(1)}, u32[]{:S(2)}, u32[]{:S(2)}) async-start(bf16[128,2,512]{2,0,1:T(8,128)(2,1)} %copy.136), calls=%async_computation.2 | async-start | bytes 524288 | tf_op jit(solution)/shard_map/all_to_all | solution.py:80
  12.7 3.4 %all-to-all-start.1 = ((bf16[128,2,512]{2,0,1:T(8,128)(2,1)}), bf16[128,2,512]{2,0,1:T(8,128)(2,1)S(1)}, u32[]{:S(2)}, u32[]{:S(2)}) async-start(bf16[128,2,512]{2,0,1:T(8,128)(2,1)} %copy.133), calls=%async_computation.1 | async-start | bytes 524288 | tf_op jit(solution)/shard_map/all_to_all | solution.py:79
  16.7 4.6 %all-to-all-done.1 = bf16[128,2,512]{2,0,1:T(8,128)(2,1)S(1)} async-done(((bf16[128,2,512]{2,0,1:T(8,128)(2,1)}), bf16[128,2,512]{2,0,1:T(8,128)(2,1)S(1)}, u32[]{:S(2)}, u32[]{:S(2)}) %all-to-all-start.1) | async-done | bytes 262176 | tf_op jit(solution)/shard_map/all_to_all | solution.py:79
  24.5 3.3 broadcast_in_dim.77
  34.8 4.4 %all-to-all-start = ((bf16[128,2,2048]{0,2,1:T(8,128)(2,1)}), bf16[128,2,2048]{0,2,1:T(8,128)(2,1)}, u32[]{:S(2)}, u32[]{:S(2)}) async-start(bf16[128,2,2048]{0,2,1:T(8,128)(2,1)} %bitcast.31), calls=%async_computation | async-start | bytes 2097152 | tf_op jit(solution)/shard_map/all_to_all | solution.py:77
  46.5 7.2 %all-to-all-done = bf16[128,2,2048]{0,2,1:T(8,128)(2,1)} async-done(((bf16[128,2,2048]{0,2,1:T(8,128)(2,1)}), bf16[128,2,2048]{0,2,1:T(8,128)(2,1)}, u32[]{:S(2)}, u32[]{:S(2)}) %all-to-all-start) | async-done | bytes 1048608 | tf_op jit(solution)/shard_map/all_to_all | solution.py:77
  53.7 4.4 %all-to-all-start.3 = ((bf16[128,2,2048]{0,2,1:T(8,128)(2,1)}), bf16[128,2,2048]{0,2,1:T(8,128)(2,1)}, u32[]{:S(2)}, u32[]{:S(2)}) async-start(bf16[128,2,2048]{0,2,1:T(8,128)(2,1)} %bitcast.41), calls=%async_computation.3 | async-start | bytes 2097152 | tf_op jit(solution)/shard_map/all_to_all | solution.py:78
  60.7 3.6 %copy.138 = bf16[4,4,128,1024]{3,2,1,0:T(8,128)(2,1)S(1)} copy(bf16[4,4,128,1024]{3,1,2,0:T(4,128)(2,1)} %constant_dynamic-update-slice_fusion.1) | data formatting | bytes 8388608 | tf_op jit(solution)/shard_map/dynamic_update_slice | solution.py:137
  64.3 14.1 %collective-permute-done.2 = bf16[1,4,128,1024]{3,1,2,0:T(4,128)(2,1)} collective-permute-done((bf16[1,4,128,1024]{3,1,2,0:T(4,128)(2,1)S(1)}, bf16[1,4,128,1024]{3,1,2,0:T(4,128)(2,1)}, u32[]{:S(2)}, u32[]{:S(2)}) %collective-permute-start.2) | collective-permute-done | bytes 1048608 | tf_op jit(solution)/shard_map/ppermute | solution.py:136
  82.6 65.8 %while.12 = (s32[]{:T(128)}, f32[2,8,128,1024]{2,3,1,0:T(8,128)}, bf16[2,128,2048]{1,2,0:T(8,128)(2,1)}, bf16[2,128,2048]{1,2,0:T(8,128)(2,1)}, s32[2,8]{1,0:T(2...) while((s32[]{:T(128)}, f32[2,8,128,1024]{2,3,1,0:T(8,128)}, ...), condition=%wide.region_7.8_spmd, body=%wide.region_3.7_spmd.sunk | while | flops 2729438208 | bytes 243889072 | solution.py:149
  97.4 5.3 %fusion.94 = (f32[4,4,128]{2,1,0:T(4,128)S(1)}, f32[4,8,128,128,4]{3,2,4,1,0:T(8,128)S(1)}) fusion(f32[4,4,128]{2,1,0:T(4,128)S(1)} %fusion.92, f32[4,4,128]{2,1,0:T(4,128)S(1)} %get-tuple-element.139, f32[4,8,128,128,4]{3,2,4,1,0:T(8,128)} %copy-done, bf16[128,4,4,128,1]{0,3,2,4,1:T(8,128)(2,1)S(1)} %bitcast.200, ...), kind=kOutput, calls=%fused_computation.3.clone.1 | convolution fusion | flops 547354624 | bytes 18374656 | tf_op jit(solution)/shard_map/while/body/eval_jaxpr/tkgd,eskd->kgtes/dot_general | solution.py:40
  130.2 5.3 %fusion.94 = (f32[4,4,128]{2,1,0:T(4,128)S(1)}, f32[4,8,128,128,4]{3,2,4,1,0:T(8,128)S(1)}) fusion(f32[4,4,128]{2,1,0:T(4,128)S(1)} %fusion.92, f32[4,4,128]{2,1,0:T(4,128)S(1)} %get-tuple-element.139, f32[4,8,128,128,4]{3,2,4,1,0:T(8,128)} %copy-done, bf16[128,4,4,128,1]{0,3,2,4,1:T(8,128)(2,1)S(1)} %bitcast.200, ...), kind=kOutput, calls=%fused_computation.3.clone.1 | convolution fusion | flops 547354624 | bytes 18374656 | tf_op jit(solution)/shard_map/while/body/eval_jaxpr/tkgd,eskd->kgtes/dot_general | solution.py:40
  148.4 8.9 %copy.143 = f32[16,128,1024]{2,0,1:T(8,128)} copy(f32[16,128,1024]{1,2,0:T(8,128)} %bitcast.205) | data formatting | bytes 16777216 | tf_op jit(solution)/shard_map/reshape | solution.py:159
  157.2 9.6 %fusion.35 = f32[18,128,1024]{2,0,1:T(8,128)S(1)} fusion(f32[16,128,1024]{2,0,1:T(8,128)} %copy.143, s32[16]{0:T(128)S(1)} %bitcast.215), kind=kOutput, calls=%fused_computation.57 | convolution fusion | flops 452985120 | bytes 17825856 | tf_op jit(solution)/shard_map/ms,mxd->sxd/dot_general | solution.py:156
  166.9 4.5 %copy-done.2 = f32[18,128,1024]{2,0,1:T(8,128)} copy-done((f32[18,128,1024]{2,0,1:T(8,128)}, f32[18,128,1024]{2,0,1:T(8,128)S(1)}, u32[]{:S(2)}) %copy-start.2) | copy-done | bytes 9437208
  171.4 5.3 %slice.29 = f32[16,128,1024]{2,0,1:T(8,128)} slice(f32[18,128,1024]{2,0,1:T(8,128)S(1)} %fusion.35), slice={[2:18], [0:128], [0:1024]} | slice | bytes 16777216 | tf_op jit(solution)/shard_map/slice | solution.py:163
  176.7 9.8 %reshape.355 = f32[4,4,128,1024]{3,1,0,2:T(4,128)} reshape(f32[16,128,1024]{2,0,1:T(8,128)} %slice.29) | data formatting | bytes 16777216 | tf_op jit(solution)/shard_map/reshape | solution.py:163
  186.5 9.4 %copy.144 = f32[4,4,128,1024]{3,1,2,0:T(4,128)} copy(f32[4,4,128,1024]{3,1,0,2:T(4,128)} %reshape.355) | data formatting | bytes 16777216 | tf_op jit(solution)/shard_map/reshape | solution.py:163
  196.0 100.7 %all_to_all.117 = f32[4,4,128,1024]{3,1,2,0:T(4,128)} all-to-all(f32[4,4,128,1024]{3,1,2,0:T(4,128)} %copy.144), channel_id=1, replica_groups=mesh['dp'=4,'ctx'=4,'uly'=2] {'ctx'}, dimensions={0} | all-to-all | bytes 16777216 | tf_op jit(solution)/shard_map/all_to_all | solution.py:166
  296.7 3.6 %all-to-all-start.4 = ((bf16[2,128,2048]{1,2,0:T(8,128)(2,1)}), bf16[2,128,2048]{1,2,0:T(8,128)(2,1)S(1)}, u32[]{:S(2)}, u32[]{:S(2)}) async-start(bf16[2,128,2048]{1,2,0:T(8,128)(2,1)} %get-tuple-element.41), calls=%async_computation.4 | async-start | bytes 2097152 | tf_op jit(solution)/shard_map/all_to_all | solution.py:174
  300.3 14.1 %fusion.29 = bf16[2,128,1024]{2,0,1:T(2,128)(2,1)S(1)} fusion(f32[4,4,128,1024]{3,1,2,0:T(4,128)} %all_to_all.117, f32[18,128,1024]{2,0,1:T(8,128)} %copy-done.2, s32[4,4,2]{1,2,0:T(2,128)S(1)} %copy-done.5), kind=kOutput, calls=%fused_computation.41 | convolution fusion | flops 50856000 | bytes 9961600 | tf_op jit(solution)/shard_map/csb,csxd->bxd/dot_general | solution.py:167
  315.4 3.4 %all-to-all-start.6 = ((bf16[2,128,512]{2,1,0:T(8,128)(2,1)}), bf16[2,128,512]{2,1,0:T(8,128)(2,1)S(1)}, u32[]{:S(2)}, u32[]{:S(2)}) async-start(bf16[2,128,512]{2,1,0:T(8,128)(2,1)} %copy.146), calls=%async_computation.6 | async-start | bytes 524288 | tf_op jit(solution)/shard_map/all_to_all | solution.py:175
  319.6 4.4 %all-to-all-done.6 = bf16[2,128,512]{2,1,0:T(8,128)(2,1)S(1)} async-done(((bf16[2,128,512]{2,1,0:T(8,128)(2,1)}), bf16[2,128,512]{2,1,0:T(8,128)(2,1)S(1)}, u32[]{:S(2)}, u32[]{:S(2)}) %all-to-all-start.6) | async-done | bytes 262176 | tf_op jit(solution)/shard_map/all_to_all | solution.py:175
  324.0 3.4 %all-to-all-start.7 = ((bf16[2,128,512]{2,1,0:T(8,128)(2,1)}), bf16[2,128,512]{2,1,0:T(8,128)(2,1)S(1)}, u32[]{:S(2)}, u32[]{:S(2)}) async-start(bf16[2,128,512]{2,1,0:T(8,128)(2,1)} %copy.148), calls=%async_computation.7 | async-start | bytes 524288 | tf_op jit(solution)/shard_map/all_to_all | solution.py:176
  (129 shorter events, 95.2 us)
Async XLA Ops:
  2.6 10.1 %all-to-all-start.2 = ((bf16[128,2,512]{2,0,1:T(8,128)(2,1)}), bf16[128,2,512]{2,0,1:T(8,128)(2,1)S(1)}, u32[]{:S(2)}, u32[]{:S(2)}) async-start(bf16[128,2,512]{2,0,1:T(8,128)(2,1)} %copy.136), calls=%async_computation.2 | async-start | bytes 524288 | tf_op jit(solution)/shard_map/all_to_all | solution.py:80
  12.7 8.6 %all-to-all-start.1 = ((bf16[128,2,512]{2,0,1:T(8,128)(2,1)}), bf16[128,2,512]{2,0,1:T(8,128)(2,1)S(1)}, u32[]{:S(2)}, u32[]{:S(2)}) async-start(bf16[128,2,512]{2,0,1:T(8,128)(2,1)} %copy.133), calls=%async_computation.1 | async-start | bytes 524288 | tf_op jit(solution)/shard_map/all_to_all | solution.py:79
  16.4 8.1 %copy-start.4 = (s32[4,4,2]{1,2,0:T(2,128)}, s32[4,4,2]{1,2,0:T(2,128)S(1)}, u32[]{:S(2)}) copy-start(s32[4,4,2]{1,2,0:T(2,128)S(1)} %convert_reduce_fusion) | copy-start | bytes 388
  30.7 13.2 %collective-permute-start = (bf16[1,4,128,1024]{3,1,2,0:T(4,128)(2,1)}, bf16[1,4,128,1024]{3,1,2,0:T(4,128)(2,1)}, u32[]{:S(2)}, u32[]{:S(2)}) collective-permute-start(bf16[1,4,128,1024]{3,1,2,0:T(4,128)(2,1)} %get-tuple-element.78), channel_id=1, source_target_pairs={{0,2},{2,0},{4,6},{6,4},{1,3},{3,1},{5,7},{7,5},{8,10},{10,8},{12,... | collective-permute-start | bytes 3145736 | tf_op jit(solution)/shard_map/ppermute | solution.py:136
  30.7 27.4 %collective-permute-start.1 = (bf16[1,4,128,1024]{3,1,2,0:T(4,128)(2,1)S(1)}, bf16[1,4,128,1024]{3,1,2,0:T(4,128)(2,1)}, u32[]{:S(2)}, u32[]{:S(2)}) collective-permute-start(bf16[1,4,128,1024]{3,1,2,0:T(4,128)(2,1)S(1)} %get-tuple-element.77), channel_id=1, source_target_pairs={{0,4},{2,6},{4,0},{6,2},{1,5},{3,7},{5,1},{7,3},{8,12},{10,14},{12... | collective-permute-start | bytes 3145736 | tf_op jit(solution)/shard_map/ppermute | solution.py:136
  32.4 46.1 %collective-permute-start.2 = (bf16[1,4,128,1024]{3,1,2,0:T(4,128)(2,1)S(1)}, bf16[1,4,128,1024]{3,1,2,0:T(4,128)(2,1)}, u32[]{:S(2)}, u32[]{:S(2)}) collective-permute-start(bf16[1,4,128,1024]{3,1,2,0:T(4,128)(2,1)S(1)} %get-tuple-element.76), channel_id=1, source_target_pairs={{0,6},{2,4},{4,2},{6,0},{1,7},{3,5},{5,3},{7,1},{8,14},{10,12},{12... | collective-permute-start | bytes 3145736 | tf_op jit(solution)/shard_map/ppermute | solution.py:136
  34.8 18.8 %all-to-all-start = ((bf16[128,2,2048]{0,2,1:T(8,128)(2,1)}), bf16[128,2,2048]{0,2,1:T(8,128)(2,1)}, u32[]{:S(2)}, u32[]{:S(2)}) async-start(bf16[128,2,2048]{0,2,1:T(8,128)(2,1)} %bitcast.31), calls=%async_computation | async-start | bytes 2097152 | tf_op jit(solution)/shard_map/all_to_all | solution.py:77
  53.7 28.9 %all-to-all-start.3 = ((bf16[128,2,2048]{0,2,1:T(8,128)(2,1)}), bf16[128,2,2048]{0,2,1:T(8,128)(2,1)}, u32[]{:S(2)}, u32[]{:S(2)}) async-start(bf16[128,2,2048]{0,2,1:T(8,128)(2,1)} %bitcast.41), calls=%async_computation.3 | async-start | bytes 2097152 | tf_op jit(solution)/shard_map/all_to_all | solution.py:78
  91.4 3.2 copy-start
  97.4 6.1 %copy-start.1 = (f32[4,8,128,128,4]{3,2,4,1,0:T(8,128)S(1)}, f32[4,8,128,128,4]{3,2,4,1,0:T(8,128)}, u32[]{:S(2)}) copy-start(f32[4,8,128,128,4]{3,2,4,1,0:T(8,128)} %copy-done) | copy-start | bytes 25165828 | tf_op jit(solution)/shard_map/while
  107.4 2.6 slice-start
  107.6 3.4 %slice-start.1 = ((s8[8388608]{0:T(1024)(128)(4,1)}), s8[4194304]{0:T(1024)(128)(4,1)S(1)}, s32[]{:S(2)}) async-start(s8[8388608]{0:T(1024)(128)(4,1)} %bitcast.203), calls=%async_computation.9 | async-start | bytes 8388608 | tf_op jit(solution)/shard_map/while
  111.4 3.2 copy-start.3
  124.3 3.2 copy-start
  130.2 6.1 %copy-start.1 = (f32[4,8,128,128,4]{3,2,4,1,0:T(8,128)S(1)}, f32[4,8,128,128,4]{3,2,4,1,0:T(8,128)}, u32[]{:S(2)}) copy-start(f32[4,8,128,128,4]{3,2,4,1,0:T(8,128)} %copy-done) | copy-start | bytes 25165828 | tf_op jit(solution)/shard_map/while
  140.3 2.6 slice-start
  140.5 3.4 %slice-start.1 = ((s8[8388608]{0:T(1024)(128)(4,1)}), s8[4194304]{0:T(1024)(128)(4,1)S(1)}, s32[]{:S(2)}) async-start(s8[8388608]{0:T(1024)(128)(4,1)} %bitcast.203), calls=%async_computation.9 | async-start | bytes 8388608 | tf_op jit(solution)/shard_map/while
  144.3 3.2 copy-start.3
  148.4 8.9 %copy-start.6 = (s32[1,16]{1,0:T(1,128)S(1)}, s32[1,16]{1,0:T(1,128)}, u32[]{:S(2)}) copy-start(s32[1,16]{1,0:T(1,128)} %get-tuple-element.67) | copy-start | bytes 196
  166.9 4.5 %copy-start.2 = (f32[18,128,1024]{2,0,1:T(8,128)}, f32[18,128,1024]{2,0,1:T(8,128)S(1)}, u32[]{:S(2)}) copy-start(f32[18,128,1024]{2,0,1:T(8,128)S(1)} %fusion.35) | copy-start | bytes 28311556
  195.9 104.3 %copy-start.5 = (s32[4,4,2]{1,2,0:T(2,128)S(1)}, s32[4,4,2]{1,2,0:T(2,128)}, u32[]{:S(2)}) copy-start(s32[4,4,2]{1,2,0:T(2,128)} %copy-done.4) | copy-start | bytes 388
  296.7 18.8 %all-to-all-start.4 = ((bf16[2,128,2048]{1,2,0:T(8,128)(2,1)}), bf16[2,128,2048]{1,2,0:T(8,128)(2,1)S(1)}, u32[]{:S(2)}, u32[]{:S(2)}) async-start(bf16[2,128,2048]{1,2,0:T(8,128)(2,1)} %get-tuple-element.41), calls=%async_computation.4 | async-start | bytes 2097152 | tf_op jit(solution)/shard_map/all_to_all | solution.py:174
  315.4 8.6 %all-to-all-start.6 = ((bf16[2,128,512]{2,1,0:T(8,128)(2,1)}), bf16[2,128,512]{2,1,0:T(8,128)(2,1)S(1)}, u32[]{:S(2)}, u32[]{:S(2)}) async-start(bf16[2,128,512]{2,1,0:T(8,128)(2,1)} %copy.146), calls=%async_computation.6 | async-start | bytes 524288 | tf_op jit(solution)/shard_map/all_to_all | solution.py:175
  324.0 8.6 %all-to-all-start.7 = ((bf16[2,128,512]{2,1,0:T(8,128)(2,1)}), bf16[2,128,512]{2,1,0:T(8,128)(2,1)S(1)}, u32[]{:S(2)}, u32[]{:S(2)}) async-start(bf16[2,128,512]{2,1,0:T(8,128)(2,1)} %copy.148), calls=%async_computation.7 | async-start | bytes 524288 | tf_op jit(solution)/shard_map/all_to_all | solution.py:176
